TPU v7x, 256 devices: a whole 4x4x8 slice. The times are simulated.
256 devices in a mesh: row: 16 (over z_lo, x, core), col: 16 (over z_hi, y).
Axes of the slice: x: 4, y: 4, z: 8 (z_hi: 4, z_lo: 2; z = z_hi * 2 + z_lo), core: 2. Of those that a mesh axis runs over, the one named last changes fastest.
Arguments:
- embeddings: bfloat16 [32768, 768], P(('row', 'col')), may hold values from -400 to 400
- tile_list: int32 [16, 16, 32, 2], P('row', 'col'), may hold values from -1 to 15, as said below
- seeds: int32 [32768], P(('row', 'col')), may hold values from 0 to 127
Outputs:
- scores: float32 [32768, 64], P(('row', 'col'))
Inputs may be any that keep to these rules, and one draw needn't show every extreme that they name: tile_list[r, c] lists the tiles of the device at row index r and column index c: a live slot (a, b) stands for the tile of document block r * 16 + a against block b * 16 + c, with a < 16, b < 16 and r * 16 + a <= b * 16 + c. Live slots come first and are distinct, empty slots hold -1 in both entries, the tile (c, r) of a block against itself is always listed, and some device fills all 32 slots. `seeds`: values of 64 or more mark a document without a seed label.
All inputs are finite; a program needn't handle non-finite values.
Results may differ from a plain program's by a relative error of at most 0.00056.
Values may be sent and summed in bfloat16 or wider, within the bound.
No kernel may reach another device: no remote copies, remote signals or barrier semaphores. Data moves between devices by JAX's collectives and lax.ppermute only.
A program may use at most 64 MiB of HBM per device.

v0:
```python
import jax
import jax.numpy as jnp
from jax import lax
from jax.experimental import pallas as pl
from jax.experimental.pallas import tpu as pltpu
from jax.sharding import Mesh
from jax.sharding import PartitionSpec as P


CLASSES = 64
BLEND = 0.8
EPSILON = 1e-06
AXES = ("zlo", "x", "core", "zhi", "y")
SIZES = (2, 4, 2, 4, 4)
ROW = ("zlo", "x", "core")
COL = ("zhi", "y")
PLANE = ("x", "y")
LINE = ("zlo", "core", "zhi")
GROUP = 16
BLOCKS = GROUP * GROUP
ROWS = 128
FEAT = 768
EXTRA = 24
LOG2_E = 1.4426950408889634
NOTHING = -10000.0
FOLDS = FEAT // ROWS
CHUNK = 32
VMEM = pl.BlockSpec(memory_space=pltpu.VMEM)
SMEM = pl.BlockSpec(memory_space=pltpu.SMEM)
ANY = pl.BlockSpec(memory_space=pl.ANY)


def position():
    x, y, zlo, core, zhi = (lax.axis_index(name) for name in ("x", "y", "zlo", "core", "zhi"))
    return x, y, zlo, core, zhi, zlo * 8 + core * 4 + zhi


def prep_kernel(emb_hbm, slots_hbm, folded_ref, copies_ref, bits_ref,
                emb_ref, slots_ref, turned_ref, emb_sem, slots_sem, out_sem):
    copies = [
        pltpu.make_async_copy(emb_hbm, emb_ref, emb_sem),
        pltpu.make_async_copy(slots_hbm, slots_ref, slots_sem),
    ]
    for copy in copies:
        copy.start()
    for copy in copies:
        copy.wait()
    features = emb_ref[...].astype(jnp.float32)
    norm = lax.rsqrt(jnp.sum(features * features, axis=1, keepdims=True) + EPSILON)
    normed = features * norm
    for k in range(FOLDS):
        part = normed[:, k * ROWS : (k + 1) * ROWS]
        folded_ref[k * ROWS : (k + 1) * ROWS, :] = part.astype(jnp.bfloat16)
        turned_ref[k * ROWS : (k + 1) * ROWS, :] = part.T.astype(jnp.bfloat16)
    sends = [pltpu.make_async_copy(turned_ref, copies_ref.at[k], out_sem) for k in range(GROUP)]
    for send in sends:
        send.start()
    first, second = slots_ref[0:1, :], slots_ref[1:2, :]
    ids = jnp.where(first >= 0, first * GROUP + second, -1)
    hits = (lax.broadcasted_iota(jnp.int32, (BLOCKS, 32), 0) == ids).astype(jnp.float32)
    bits = lax.dot_general(
        jnp.ones((8, 32), jnp.float32), hits, (((1,), (1,)), ((), ())),
        preferred_element_type=jnp.float32,
    )
    row = lax.broadcasted_iota(jnp.int32, (8, ROWS), 0)
    halves = jnp.where(row < 4, bits[:, :ROWS], bits[:, ROWS:]).astype(jnp.bfloat16)
    bits_ref[...] = halves
    for send in sends:
        send.wait()


def relay_kernel(folded_ref, seeds_ref, bits_ref, *refs):
    x, y, *_ = position()
    out_ref = refs[6]
    out_ref[:FEAT, :] = folded_ref[...]
    row = lax.broadcasted_iota(jnp.int32, (8, ROWS), 0)
    groups = []
    for own, others in ((x, refs[:3]), (y, refs[3:6])):
        rows = jnp.zeros((8, ROWS), jnp.float32)
        for step, ref in enumerate((bits_ref, *others)):
            at = 2 * (own ^ step)
            note = ref[...].astype(jnp.float32)
            rows = jnp.where(row == at, note[0:1], jnp.where(row == at + 1, note[4:5], rows))
        groups.append(rows)
    groups.append(jnp.broadcast_to(seeds_ref[...].astype(jnp.float32), (8, ROWS)))
    out_ref[FEAT:, :] = jnp.concatenate(groups, axis=0).astype(jnp.bfloat16)


def make_list(notes, list_v):
    x, y, zlo, core, zhi, mine = position()
    shape = (BLOCKS, BLOCKS)
    row = lax.broadcasted_iota(jnp.int32, shape, 0)
    lane = lax.broadcasted_iota(jnp.int32, shape, 1)
    u_zhi, u_x = row >> 6, (row >> 4) & 3
    v_zlo, v_core, v_y = (row >> 3) & 1, (row >> 2) & 1, row & 3
    a_zhi, a_y = lane >> 6, (lane >> 4) & 3
    b_zlo, b_x, b_core = (lane >> 3) & 1, (lane >> 1) & 3, lane & 1
    forward = (a_zhi == zhi) & (b_x == x) & (a_y == v_y) & (b_zlo == v_zlo) & (b_core == v_core)
    mirror = (a_zhi == u_zhi) & (a_y == y) & (b_zlo == zlo) & (b_x == u_x) & (b_core == core)
    ahead, back = [], []
    for part in range(4):
        note = notes[part].astype(jnp.float32)
        for k in range(4):
            full = jnp.concatenate([note[2 * k : 2 * k + 1], note[2 * k + 1 : 2 * k + 2]], axis=1)
            ahead.append(jnp.broadcast_to(full, (GROUP, BLOCKS)))
        note = notes[(part ^ (mine >> 2)) * 4 + zhi].astype(jnp.float32)
        for k in range(4, 8):
            full = jnp.concatenate([note[2 * k : 2 * k + 1], note[2 * k + 1 : 2 * k + 2]], axis=1)
            back.append(full)
    ahead = jnp.concatenate(ahead, axis=0)
    back = jnp.concatenate(back * GROUP, axis=0)
    hits = jnp.where(forward, ahead, 0.0) + jnp.where(mirror, back, 0.0)
    counts = jnp.dot(
        hits.astype(jnp.bfloat16), jnp.ones(shape, jnp.bfloat16), preferred_element_type=jnp.float32
    )
    live = (counts > 0.0).astype(jnp.float32)
    upto = jnp.dot(
        (lane <= row).astype(jnp.float32).astype(jnp.bfloat16), live.astype(jnp.bfloat16),
        preferred_element_type=jnp.float32,
    )
    spot = jnp.where(lane.astype(jnp.float32) == upto - 1.0, live, 0.0)
    slot_lane = lax.broadcasted_iota(jnp.int32, (8, BLOCKS), 1)
    code = (
        (((slot_lane >> 4) & 3) * 4 + (slot_lane & 3)) * GROUP
        + ((slot_lane >> 3) & 1) * 8 + ((slot_lane >> 2) & 1) * 4 + (slot_lane >> 6)
    ).astype(jnp.float32).astype(jnp.bfloat16)
    ones = jnp.ones((8, BLOCKS), jnp.bfloat16)
    codes = jnp.dot(code, spot.astype(jnp.bfloat16), preferred_element_type=jnp.float32)
    weights = jnp.dot(ones, (spot * counts).astype(jnp.bfloat16), preferred_element_type=jnp.float32)
    found = jnp.dot(ones, live.astype(jnp.bfloat16), preferred_element_type=jnp.float32)
    line = lax.broadcasted_iota(jnp.int32, (8, BLOCKS), 0)
    diag = jnp.where(codes == ((x * 4 + y) * GROUP + mine).astype(jnp.float32), weights, 0.0)
    spots = jnp.where(diag > 0.0, slot_lane.astype(jnp.float32), 0.0)
    spot_at = jnp.broadcast_to(jnp.sum(spots, axis=1, keepdims=True), spots.shape)
    tail = jnp.where(line == 2, found, spot_at)
    table = jnp.where(line == 0, codes, jnp.where(line == 1, weights - diag, tail))
    list_v[...] = (table + 0.5).astype(jnp.int32)


def unfold(blocks, at):
    return jnp.concatenate([blocks[at, f * ROWS : (f + 1) * ROWS, :] for f in range(FOLDS)], axis=1)


def build_kernel(plane_ref, own_ref, mate_ref, far_ref, far_mate_ref,
                 tiles_ref, list_ref, deg_ref, seeds_ref, line_v, notes, sums, list_v, list_sem, line_sem, notes_sem):
    x, y, *_, mine = position()
    planes = mine & 12
    arrays = tuple(enumerate((own_ref, mate_ref, far_ref, far_mate_ref)))
    extras = [
        pltpu.make_async_copy(
            part.at[:, pl.ds(FEAT, EXTRA)], notes.at[pl.ds(at * 4, 4)], notes_sem
        )
        for at, part in arrays
    ]
    parts = [
        pltpu.make_async_copy(part.at[:, pl.ds(0, FEAT)], line_v.at[pl.ds(at * 4, 4)], line_sem)
        for at, part in arrays
    ]
    for copy in extras + parts:
        copy.start()
    for copy in extras:
        copy.wait()
    make_list(notes, list_v)
    list_copy = pltpu.make_async_copy(list_v, list_ref, list_sem)
    list_copy.start()
    for b in range(GROUP):
        seeds_ref[b : b + 1, :] = notes[b ^ planes, GROUP:, :].astype(jnp.float32)[0:1].astype(jnp.int32)
    sums[...] = jnp.zeros_like(sums)
    sharpness = FEAT**0.5 * LOG2_E
    list_copy.wait()
    for part in parts:
        part.wait()

    def scores(a, b):
        return jnp.dot(
            unfold(line_v, b ^ planes), plane_ref[a], preferred_element_type=jnp.float32
        )

    def build_chunk(group, carry):
        for k in range(CHUNK):
            at = group * CHUNK + k
            slot = list_ref[0, at]
            a, b = slot >> 4, slot & 15
            offset = jnp.where(list_ref[1, at] > 0, -sharpness, NOTHING)
            tile = jnp.exp2(sharpness * scores(a, b) + offset)
            tiles_ref[at] = tile.astype(jnp.bfloat16)
            sums[b] += tile
        return carry

    lax.fori_loop(0, (list_ref[2, 0] + CHUNK - 1) // CHUNK, build_chunk, 0)
    off_diag = (
        lax.broadcasted_iota(jnp.int32, (ROWS, ROWS), 0)
        != lax.broadcasted_iota(jnp.int32, (ROWS, ROWS), 1)
    )
    tile = 2.0 * jnp.exp2(sharpness * scores(x * 4 + y, mine) - sharpness)
    tile = jnp.where(off_diag, tile, 0.0)
    tiles_ref[list_ref[3, 0]] = tile.astype(jnp.bfloat16)
    sums[mine] += tile
    for b in range(GROUP):
        deg_ref[b : b + 1, :] = jnp.sum(sums[b].T, axis=0, keepdims=True)


def run_apply(list_ref, tiles_ref, out_ref, total, spread):
    total[...] = jnp.zeros_like(total)

    def chunk_step(group, carry):
        for k in range(CHUNK):
            at = group * CHUNK + k
            slot = list_ref[0, at]
            total[slot >> 4] += jnp.dot(
                spread[slot & 15], tiles_ref[at], preferred_element_type=jnp.float32
            )
        return carry

    lax.fori_loop(0, (list_ref[2, 0] + CHUNK - 1) // CHUNK, chunk_step, 0)
    out_ref[...] = total[...].astype(jnp.bfloat16)


def seeded_block(seeds_ref, b):
    classes = lax.broadcasted_iota(jnp.int32, (CLASSES, ROWS), 0)
    return classes == seeds_ref[b : b + 1, :]


def first_kernel(list_ref, tiles_ref, seeds_ref, parts_ref,
                 out_ref, scale_ref, own_ref, total, spread):
    scale_ref[...] = lax.rsqrt(jnp.sum(parts_ref[...], axis=0))
    own_ref[...] = scale_ref[pl.ds(position()[5], 1), :]
    for b in range(GROUP):
        seeded = jnp.where(seeded_block(seeds_ref, b), scale_ref[b : b + 1, :], 0.0)
        spread[b] = seeded.astype(jnp.bfloat16)
    run_apply(list_ref, tiles_ref, out_ref, total, spread)


def next_kernel(list_ref, tiles_ref, seeds_ref, scale_ref, own_ref, mate_ref,
                out_ref, total, spread):
    core = lax.axis_index("core")
    classes = lax.broadcasted_iota(jnp.int32, (CLASSES, ROWS), 0)
    for k in range(GROUP // 2):
        for smooth_ref, side in ((own_ref, core), (mate_ref, 1 - core)):
            b = (k // 4) * 8 + side * 4 + k % 4
            seeded = classes == seeds_ref[pl.ds(b, 1), :]
            seed_part = jnp.where(seeded, (1.0 - BLEND) * scale_ref[pl.ds(b, 1), :], 0.0)
            spread[b] = (smooth_ref[k].astype(jnp.float32) + seed_part).astype(jnp.bfloat16)
    run_apply(list_ref, tiles_ref, out_ref, total, spread)


def call(kernel, outs, ins, out_specs, scratch=(), limit=8):
    return pl.pallas_call(
        kernel,
        out_shape=outs,
        in_specs=ins,
        out_specs=out_specs,
        scratch_shapes=list(scratch),
        compiler_params=pltpu.CompilerParams(vmem_limit_bytes=limit << 20),
    )


def array(*shape, dtype=jnp.float32):
    return jax.ShapeDtypeStruct(shape, dtype)


def exchange(blocks, axes):
    return lax.all_to_all(blocks, axes, 0, 0)


def gather(block, axes, count=GROUP):
    return exchange(jnp.broadcast_to(block[None], (count,) + block.shape), axes)


def pairs(count, step):
    return [(k, k ^ step) for k in range(count)]


def local(embeddings, tile_list, seeds):
    folded, copies, bits = call(
        prep_kernel,
        (
            array(FEAT, ROWS, dtype=jnp.bfloat16),
            array(GROUP, FEAT, ROWS, dtype=jnp.bfloat16),
            array(8, ROWS, dtype=jnp.bfloat16),
        ),
        [ANY] * 2,
        (VMEM, ANY, VMEM),
        (
            pltpu.VMEM((ROWS, FEAT), jnp.bfloat16),
            pltpu.VMEM((2, 32), jnp.int32),
            pltpu.VMEM((FEAT, ROWS), jnp.bfloat16),
            pltpu.SemaphoreType.DMA,
            pltpu.SemaphoreType.DMA,
            pltpu.SemaphoreType.DMA,
        ),
        limit=60,
    )(embeddings, tile_list.reshape(-1, 2).T)
    others = []
    for axis in PLANE:
        for step in (1, 2, 3):
            others.append(lax.ppermute(bits, axis, pairs(4, step)))
    plane = exchange(copies, PLANE)
    block = call(
        relay_kernel,
        array(FEAT + EXTRA, ROWS, dtype=jnp.bfloat16),
        [VMEM] * 9,
        VMEM,
        limit=4,
    )(folded, seeds[None, :], bits, *others)
    own = pltpu.with_memory_space_constraint(lax.all_gather(block, "zhi"), pltpu.HBM)
    far = lax.ppermute(own, "zlo", pairs(2, 1))
    mate = lax.ppermute(own, "core", pairs(2, 1))
    far, mate = lax.optimization_barrier((far, mate))
    far_mate = lax.ppermute(far, "core", pairs(2, 1))

    tiles, listing, partial_degree, line_seeds = call(
        build_kernel,
        (
            array(BLOCKS, ROWS, ROWS, dtype=jnp.bfloat16),
            array(8, BLOCKS, dtype=jnp.int32),
            array(GROUP, ROWS),
            array(GROUP, ROWS, dtype=jnp.int32),
        ),
        [VMEM] + [ANY] * 4,
        (VMEM, SMEM, VMEM, VMEM),
        (
            pltpu.VMEM((GROUP, FEAT, ROWS), jnp.bfloat16),
            pltpu.VMEM((GROUP, EXTRA, ROWS), jnp.bfloat16),
            pltpu.VMEM((GROUP, ROWS, ROWS), jnp.float32),
            pltpu.VMEM((8, BLOCKS), jnp.int32),
            pltpu.SemaphoreType.DMA,
            pltpu.SemaphoreType.DMA,
            pltpu.SemaphoreType.DMA,
        ),
        limit=14,
    )(plane, own, mate, far, far_mate)

    scratch = (
        pltpu.VMEM((GROUP, CLASSES, ROWS), jnp.float32),
        pltpu.VMEM((GROUP, CLASSES, ROWS), jnp.bfloat16),
    )
    sums_out = array(GROUP, CLASSES, ROWS, dtype=jnp.bfloat16)
    partial, scale, own_scale = call(
        first_kernel,
        (sums_out, array(GROUP, ROWS), array(1, ROWS)),
        [SMEM, VMEM, VMEM, VMEM],
        (VMEM,) * 3,
        scratch,
        limit=6,
    )(listing, tiles, line_seeds, gather(partial_degree, LINE))
    for sweep in range(3):
        if sweep:
            smooth = (BLEND * own_scale * own_scale * summed).astype(jnp.bfloat16)
            smooth = gather(smooth, ("zlo", "zhi"), GROUP // 2)
            partial = call(
                next_kernel, sums_out, [SMEM] + [VMEM] * 5, VMEM, scratch, limit=6
            )(listing, tiles, line_seeds, scale, smooth, lax.ppermute(smooth, "core", pairs(2, 1)))
        summed, own_scale, seeds = lax.optimization_barrier((exchange(partial, PLANE), own_scale, seeds))
        summed = jnp.sum(summed.astype(jnp.float32), axis=0)
    seeded = seeds[None, :] == jnp.arange(CLASSES, dtype=jnp.int32)[:, None]
    labels = BLEND * own_scale * summed + (1.0 - BLEND) * seeded.astype(jnp.float32)
    return (CLASSES * labels).T


def solution(mesh):
    fine = Mesh(mesh.devices.reshape(SIZES), AXES)
    return jax.shard_map(
        local,
        mesh=fine,
        in_specs=(P(AXES, None), P(ROW, COL, None, None), P(AXES)),
        out_specs=P(AXES, None),
        check_vma=False,
    )
```

profile of v0, /device:TPU:32, one launch (start us, length us, event | category | flops | bytes accessed | tf_op | source)
XLA Modules:
  0.0 190.5 jit_solution(8258879098549746772)
XLA Ops:
  0.0 3.5 %shard_map.37 = (bf16[768,128]{1,0:T(8,128)(2,1)}, bf16[16,768,128]{2,1,0:T(8,128)(2,1)}, bf16[8,128]{1,0:T(8,128)(2,1)}) custom-call(bf16[128,768]{1,0:T(8,128)(2,1)} %emb_hbm.1, s32[2,32]{1,0:T(2,128)} %bitcast.19), custom_call_target="tpu_custom_call" | custom-call | tf_op jit(solution)/shard_map/pallas_call | solution.py:275
  3.5 0.0 copy-start.1
  3.5 0.0 copy-start
  3.5 0.0 copy-start.2
  3.5 7.2 %all-to-all-start = ((bf16[16,768,128]{2,1,0:T(8,128)(2,1)}), bf16[16,768,128]{2,1,0:T(8,128)(2,1)S(1)}, u32[]{:S(2)}, u32[]{:S(2)}) async-start(bf16[16,768,128]{2,1,0:T(8,128)(2,1)} %get-tuple-element.26), calls=%async_computation | async-start | bytes 6291456 | tf_op jit(solution)/shard_map/all_to_all | solution.py:263
  10.7 0.0 copy-done.1
  10.7 3.2 %collective-permute-start.5 = (bf16[8,128]{1,0:T(8,128)(2,1)S(1)}, bf16[8,128]{1,0:T(8,128)(2,1)S(1)}, u32[]{:S(2)}, u32[]{:S(2)}) collective-permute-start(bf16[8,128]{1,0:T(8,128)(2,1)S(1)} %copy-done.1), channel_id=1, source_target_pairs={{0,3},{1,2},{2,1},{3,0},{4,7},{5,6},{6,5},{7,4},{8,11},{9,10},{10,... | collective-permute-start | bytes 6152 | tf_op jit(solution)/shard_map/ppermute | solution.py:297
  14.0 0.9 collective-permute-start.4
  14.8 0.1 collective-permute-start.3
  14.9 3.1 %collective-permute-start.2 = (bf16[8,128]{1,0:T(8,128)(2,1)S(1)}, bf16[8,128]{1,0:T(8,128)(2,1)S(1)}, u32[]{:S(2)}, u32[]{:S(2)}) collective-permute-start(bf16[8,128]{1,0:T(8,128)(2,1)S(1)} %copy-done.1), channel_id=1, source_target_pairs={{0,96},{32,64},{64,32},{96,0},{1,97},{33,65},{65,33},{97,1},{2,98}... | collective-permute-start | bytes 6152 | tf_op jit(solution)/shard_map/ppermute | solution.py:297
  18.1 0.9 collective-permute-start.1
  18.9 16.4 %collective-permute-done.5.refs_5_ = bf16[8,128]{1,0:T(8,128)(2,1)S(1)} collective-permute-done((bf16[8,128]{1,0:T(8,128)(2,1)S(1)}, bf16[8,128]{1,0:T(8,128)(2,1)S(1)}, u32[]{:S(2)}, u32[]{:S(2)}) %collective-permute-start.5) | collective-permute-done | bytes 2080 | tf_op jit(solution)/shard_map/ppermute | solution.py:297
  35.4 7.4 %collective-permute-start = (bf16[8,128]{1,0:T(8,128)(2,1)S(1)}, bf16[8,128]{1,0:T(8,128)(2,1)S(1)}, u32[]{:S(2)}, u32[]{:S(2)}) collective-permute-start(bf16[8,128]{1,0:T(8,128)(2,1)S(1)} %copy-done.1), channel_id=1, source_target_pairs={{0,32},{32,0},{64,96},{96,64},{1,33},{33,1},{65,97},{97,65},{2,34}... | collective-permute-start | bytes 6152 | tf_op jit(solution)/shard_map/ppermute | solution.py:297
  42.8 0.0 collective-permute-done.4.refs_4_
  42.8 0.0 collective-permute-done.3.refs_3_
  42.8 4.4 %collective-permute-done.2.refs_2_ = bf16[8,128]{1,0:T(8,128)(2,1)S(1)} collective-permute-done((bf16[8,128]{1,0:T(8,128)(2,1)S(1)}, bf16[8,128]{1,0:T(8,128)(2,1)S(1)}, u32[]{:S(2)}, u32[]{:S(2)}) %collective-permute-start.2) | collective-permute-done | bytes 2080 | tf_op jit(solution)/shard_map/ppermute | solution.py:297
  47.2 5.3 %collective-permute-done.1.refs_1_ = bf16[8,128]{1,0:T(8,128)(2,1)S(1)} collective-permute-done((bf16[8,128]{1,0:T(8,128)(2,1)S(1)}, bf16[8,128]{1,0:T(8,128)(2,1)S(1)}, u32[]{:S(2)}, u32[]{:S(2)}) %collective-permute-start.1) | collective-permute-done | bytes 2080 | tf_op jit(solution)/shard_map/ppermute | solution.py:297
  52.5 0.0 collective-permute-done.refs_0_
  52.5 0.0 copy-done
  52.5 0.0 copy-done.2
  52.5 21.3 %all-gather = bf16[3168,128]{1,0:T(8,128)(2,1)S(1)} all-gather(bf16[792,128]{1,0:T(8,128)(2,1)S(1)} %shard_map.38), channel_id=2, replica_groups=mesh['zlo'=2,'x'=4,'core'=2,'zhi'=4,'y'=4] {'zhi'}, dimensions={0}, use_global_device_ids=true | all-gather | bytes 1013760 | tf_op jit(solution)/shard_map/all_gather | solution.py:306
  73.8 0.0 copy-start.3
  73.8 0.0 collective-permute-start.7
  73.8 1.9 collective-permute-start.6
  75.7 0.5 collective-permute-done.7.mate_ref
  76.1 0.0 copy-start.4
  76.1 18.3 %collective-permute-done.6.far_ref = bf16[4,792,128]{2,1,0:T(8,128)(2,1)S(1)} collective-permute-done((bf16[4,792,128]{2,1,0:T(8,128)(2,1)S(1)}, bf16[4,792,128]{2,1,0:T(8,128)(2,1)S(1)}, u32[]{:S(2)}, u32[]{:S(2)}) %collective-permute-start.6) | collective-permute-done | bytes 811040 | tf_op jit(solution)/shard_map/ppermute | solution.py:307
  94.4 0.0 collective-permute-start.8
  94.4 0.0 copy-done.3
  94.4 0.0 copy-done.4
  94.4 0.9 copy-done.5
  95.3 1.5 collective-permute-done.8.far_mate_ref
  96.8 0.0 all-to-all-done.plane_ref
  96.8 7.5 %shard_map.39 = (bf16[256,128,128]{2,1,0:T(8,128)(2,1)S(1)}, s32[8,256]{1,0:T(8,128)S(1)}, f32[16,128]{1,0:T(8,128)S(1)}, s32[16,128]{1,0:T(8,128)S(1)}) custom-call(bf16[16,768,128]{2,1,0:T(8,128)(2,1)S(1)} %all-to-all-done.plane_ref, bf16[4,792,128]{2,1,0:T(8,128)(2,1)} %bitcast.18, bf16[4,792,128]{2,1,0:T(8,128)(2,1)} %copy-done.4, ...), custom_call_target="tpu_custom_call" | custom-call | tf_op jit(solution)/shard_map/pallas_call | solution.py:312
  104.3 13.7 %all_to_all.35.parts_ref = f32[16,16,128]{2,1,0:T(8,128)S(1)} all-to-all(f32[16,16,128]{2,1,0:T(8,128)S(1)} %broadcast_in_dim.9), channel_id=1, replica_groups=mesh['zlo'=2,'x'=4,'core'=2,'zhi'=4,'y'=4] {'zlo','core','zhi'}, dimensions={0} | all-to-all | bytes 262144 | tf_op jit(solution)/shard_map/all_to_all | solution.py:263
  118.0 1.6 shard_map.40
  119.7 17.1 %all_to_all.36 = bf16[16,64,128]{2,1,0:T(8,128)(2,1)S(1)} all-to-all(bf16[16,64,128]{2,1,0:T(8,128)(2,1)S(1)} %get-tuple-element.36), channel_id=1, replica_groups=mesh['zlo'=2,'x'=4,'core'=2,'zhi'=4,'y'=4] {'x','y'}, dimensions={0} | all-to-all | bytes 524288 | tf_op jit(solution)/shard_map/all_to_all | solution.py:263
  136.9 10.7 %all_to_all.37.own_ref = bf16[8,64,128]{2,1,0:T(8,128)(2,1)S(1)} all-to-all(bf16[8,64,128]{2,1,0:T(8,128)(2,1)S(1)} %broadcast_in_dim.10), channel_id=1, replica_groups=mesh['zlo'=2,'x'=4,'core'=2,'zhi'=4,'y'=4] {'zlo','zhi'}, dimensions={0} | all-to-all | bytes 262144 | tf_op jit(solution)/shard_map/all_to_all | solution.py:263
  147.7 0.0 collective-permute-start.9
  147.7 1.3 collective-permute-done.9.mate_ref
  149.0 1.7 shard_map.41
  150.7 12.7 %all_to_all.38 = bf16[16,64,128]{2,1,0:T(8,128)(2,1)S(1)} all-to-all(bf16[16,64,128]{2,1,0:T(8,128)(2,1)S(1)} %shard_map.41), channel_id=1, replica_groups=mesh['zlo'=2,'x'=4,'core'=2,'zhi'=4,'y'=4] {'x','y'}, dimensions={0} | all-to-all | bytes 524288 | tf_op jit(solution)/shard_map/all_to_all | solution.py:263
  163.4 10.7 %all_to_all.39.own_ref = bf16[8,64,128]{2,1,0:T(8,128)(2,1)S(1)} all-to-all(bf16[8,64,128]{2,1,0:T(8,128)(2,1)S(1)} %broadcast_in_dim.11), channel_id=1, replica_groups=mesh['zlo'=2,'x'=4,'core'=2,'zhi'=4,'y'=4] {'zlo','zhi'}, dimensions={0} | all-to-all | bytes 262144 | tf_op jit(solution)/shard_map/all_to_all | solution.py:263
  174.2 0.0 collective-permute-start.10
  174.2 1.3 collective-permute-done.10.mate_ref
  175.5 1.7 shard_map.42
  177.2 12.7 %all_to_all.40 = bf16[16,64,128]{2,1,0:T(8,128)(2,1)S(1)} all-to-all(bf16[16,64,128]{2,1,0:T(8,128)(2,1)S(1)} %shard_map.42), channel_id=1, replica_groups=mesh['zlo'=2,'x'=4,'core'=2,'zhi'=4,'y'=4] {'x','y'}, dimensions={0} | all-to-all | bytes 524288 | tf_op jit(solution)/shard_map/all_to_all | solution.py:263
  189.9 0.6 fusion
  (13 shorter events, 0.2 us)
Async XLA Ops:
  3.5 7.2 %copy-start.1 = (bf16[8,128]{1,0:T(8,128)(2,1)S(1)}, bf16[8,128]{1,0:T(8,128)(2,1)}, u32[]{:S(2)}) copy-start(bf16[8,128]{1,0:T(8,128)(2,1)} %get-tuple-element.28.bits_ref) | copy-start | bytes 6148
  3.5 49.0 %copy-start = (bf16[768,128]{1,0:T(8,128)(2,1)S(1)}, bf16[768,128]{1,0:T(8,128)(2,1)}, u32[]{:S(2)}) copy-start(bf16[768,128]{1,0:T(8,128)(2,1)} %get-tuple-element.27.folded_ref) | copy-start | bytes 589828
  3.5 48.9 %copy-start.2 = (s32[128]{0:T(128)S(1)}, s32[128]{0:T(128)}, u32[]{:S(2)}) copy-start(s32[128]{0:T(128)} %param.5) | copy-start | bytes 1540
  3.5 93.3 %all-to-all-start = ((bf16[16,768,128]{2,1,0:T(8,128)(2,1)}), bf16[16,768,128]{2,1,0:T(8,128)(2,1)S(1)}, u32[]{:S(2)}, u32[]{:S(2)}) async-start(bf16[16,768,128]{2,1,0:T(8,128)(2,1)} %get-tuple-element.26), calls=%async_computation | async-start | bytes 6291456 | tf_op jit(solution)/shard_map/all_to_all | solution.py:263
  10.7 24.6 %collective-permute-start.5 = (bf16[8,128]{1,0:T(8,128)(2,1)S(1)}, bf16[8,128]{1,0:T(8,128)(2,1)S(1)}, u32[]{:S(2)}, u32[]{:S(2)}) collective-permute-start(bf16[8,128]{1,0:T(8,128)(2,1)S(1)} %copy-done.1), channel_id=1, source_target_pairs={{0,3},{1,2},{2,1},{3,0},{4,7},{5,6},{6,5},{7,4},{8,11},{9,10},{10,... | collective-permute-start | bytes 6152 | tf_op jit(solution)/shard_map/ppermute | solution.py:297
  14.0 28.8 %collective-permute-start.4 = (bf16[8,128]{1,0:T(8,128)(2,1)S(1)}, bf16[8,128]{1,0:T(8,128)(2,1)S(1)}, u32[]{:S(2)}, u32[]{:S(2)}) collective-permute-start(bf16[8,128]{1,0:T(8,128)(2,1)S(1)} %copy-done.1), channel_id=1, source_target_pairs={{0,2},{1,3},{2,0},{3,1},{4,6},{5,7},{6,4},{7,5},{8,10},{9,11},{10,... | collective-permute-start | bytes 6152 | tf_op jit(solution)/shard_map/ppermute | solution.py:297
  14.8 28.0 %collective-permute-start.3 = (bf16[8,128]{1,0:T(8,128)(2,1)S(1)}, bf16[8,128]{1,0:T(8,128)(2,1)S(1)}, u32[]{:S(2)}, u32[]{:S(2)}) collective-permute-start(bf16[8,128]{1,0:T(8,128)(2,1)S(1)} %copy-done.1), channel_id=1, source_target_pairs={{0,1},{1,0},{2,3},{3,2},{4,5},{5,4},{6,7},{7,6},{8,9},{9,8},{10,11... | collective-permute-start | bytes 6152 | tf_op jit(solution)/shard_map/ppermute | solution.py:297
  14.9 32.2 %collective-permute-start.2 = (bf16[8,128]{1,0:T(8,128)(2,1)S(1)}, bf16[8,128]{1,0:T(8,128)(2,1)S(1)}, u32[]{:S(2)}, u32[]{:S(2)}) collective-permute-start(bf16[8,128]{1,0:T(8,128)(2,1)S(1)} %copy-done.1), channel_id=1, source_target_pairs={{0,96},{32,64},{64,32},{96,0},{1,97},{33,65},{65,33},{97,1},{2,98}... | collective-permute-start | bytes 6152 | tf_op jit(solution)/shard_map/ppermute | solution.py:297
  18.1 34.4 %collective-permute-start.1 = (bf16[8,128]{1,0:T(8,128)(2,1)S(1)}, bf16[8,128]{1,0:T(8,128)(2,1)S(1)}, u32[]{:S(2)}, u32[]{:S(2)}) collective-permute-start(bf16[8,128]{1,0:T(8,128)(2,1)S(1)} %copy-done.1), channel_id=1, source_target_pairs={{0,64},{32,96},{64,0},{96,32},{1,65},{33,97},{65,1},{97,33},{2,66}... | collective-permute-start | bytes 6152 | tf_op jit(solution)/shard_map/ppermute | solution.py:297
  35.4 17.1 %collective-permute-start = (bf16[8,128]{1,0:T(8,128)(2,1)S(1)}, bf16[8,128]{1,0:T(8,128)(2,1)S(1)}, u32[]{:S(2)}, u32[]{:S(2)}) collective-permute-start(bf16[8,128]{1,0:T(8,128)(2,1)S(1)} %copy-done.1), channel_id=1, source_target_pairs={{0,32},{32,0},{64,96},{96,64},{1,33},{33,1},{65,97},{97,65},{2,34}... | collective-permute-start | bytes 6152 | tf_op jit(solution)/shard_map/ppermute | solution.py:297
  73.8 20.6 %copy-start.3 = (bf16[3168,128]{1,0:T(8,128)(2,1)}, bf16[3168,128]{1,0:T(8,128)(2,1)S(1)}, u32[]{:S(2)}) copy-start(bf16[3168,128]{1,0:T(8,128)(2,1)S(1)} %all-gather) | copy-start | bytes 2433028
  73.8 2.3 %collective-permute-start.7 = (bf16[4,792,128]{2,1,0:T(8,128)(2,1)S(1)}, bf16[4,792,128]{2,1,0:T(8,128)(2,1)S(1)}, u32[]{:S(2)}, u32[]{:S(2)}) collective-permute-start(bf16[4,792,128]{2,1,0:T(8,128)(2,1)S(1)} %bitcast.16), channel_id=1, source_target_pairs={{0,16},{16,0},{1,17},{17,1},{2,18},{18,2},{3,19},{19,3},{4,20},{20... | collective-permute-start | bytes 2433032 | tf_op jit(solution)/shard_map/ppermute | solution.py:308
  73.8 20.6 %collective-permute-start.6 = (bf16[4,792,128]{2,1,0:T(8,128)(2,1)S(1)}, bf16[4,792,128]{2,1,0:T(8,128)(2,1)S(1)}, u32[]{:S(2)}, u32[]{:S(2)}) collective-permute-start(bf16[4,792,128]{2,1,0:T(8,128)(2,1)S(1)} %bitcast.17), channel_id=1, source_target_pairs={{0,128},{128,0},{1,129},{129,1},{2,130},{130,2},{3,131},{131,3},{4... | collective-permute-start | bytes 2433032 | tf_op jit(solution)/shard_map/ppermute | solution.py:307
  76.1 18.3 %copy-start.4 = (bf16[4,792,128]{2,1,0:T(8,128)(2,1)}, bf16[4,792,128]{2,1,0:T(8,128)(2,1)S(1)}, u32[]{:S(2)}) copy-start(bf16[4,792,128]{2,1,0:T(8,128)(2,1)S(1)} %collective-permute-done.7.mate_ref) | copy-start | bytes 2433028
  94.4 0.9 copy-start.5
  94.4 2.5 %collective-permute-start.8 = (bf16[4,792,128]{2,1,0:T(8,128)(2,1)S(1)}, bf16[4,792,128]{2,1,0:T(8,128)(2,1)}, u32[]{:S(2)}, u32[]{:S(2)}) collective-permute-start(bf16[4,792,128]{2,1,0:T(8,128)(2,1)S(1)} %collective-permute-done.6.far_ref), channel_id=1, source_target_pairs={{0,16},{16,0},{1,17},{17,1},{2,18},{18,2},{3,19},{19,3},{4,20},{20... | collective-permute-start | bytes 2433032 | tf_op jit(solution)/shard_map/ppermute | solution.py:310
  147.7 1.3 collective-permute-start.9
  174.2 1.3 collective-permute-start.10
where the time goes:
time: 191 us
  blocking collectives  98.9 us (52%)
  waiting for transfers between devices  49.1 us (26%)
  starting transfers between devices  24.6 us (13%)
  Pallas kernels  16 us (8%)
    all_to_all x6, blocking collectives, exchange(): return lax.all_to_all(blocks, axes, 0, 0)  77.6 us
    ppermute x6, waiting for transfers between devices, local(): others.append(lax.ppermute(bits, axis, pairs(4, step)))  26.1 us
    all_gather x1, blocking collectives, local(): lax.all_gather(block, 'zhi')  21.3 us
    ppermute x1, waiting for transfers between devices, local(): far = lax.ppermute(own, 'zlo', pairs(2, 1))  18.3 us
    ppermute x6, starting transfers between devices, local(): others.append(lax.ppermute(bits, axis, pairs(4, step)))  15.6 us
    pallas_call x1, Pallas kernels, local(): call(build_kernel, (array(BLOCKS, ROWS, ROWS, dtype=jnp.bfloat16), array(...  7.47 us
    all_to_all x1, starting transfers between devices, exchange(): return lax.all_to_all(blocks, axes, 0, 0)  7.18 us
  transfers between devices with their start and end apart: 12, of which 8 were waited for; matrix products, arithmetic and copies ran while one was open for 0% of the time, Pallas kernels for 0%

commit v1 on v0

--- a/solution.py
+++ b/solution.py
@@ -196,8 +196,8 @@
     tile = jnp.where(off_diag, tile, 0.0)
     tiles_ref[list_ref[3, 0]] = tile.astype(jnp.bfloat16)
     sums[mine] += tile
-    for b in range(GROUP):
-        deg_ref[b : b + 1, :] = jnp.sum(sums[b].T, axis=0, keepdims=True)
+    rows = [jnp.sum(sums[b].T, axis=0, keepdims=True) for b in range(GROUP)]
+    deg_ref[...] = jnp.concatenate(rows, axis=0).astype(jnp.bfloat16)
 
 
 def run_apply(list_ref, tiles_ref, out_ref, total, spread):
@@ -223,7 +223,7 @@
 
 def first_kernel(list_ref, tiles_ref, seeds_ref, parts_ref,
                  out_ref, scale_ref, own_ref, total, spread):
-    scale_ref[...] = lax.rsqrt(jnp.sum(parts_ref[...], axis=0))
+    scale_ref[...] = lax.rsqrt(jnp.sum(parts_ref[...].astype(jnp.float32), axis=0))
     own_ref[...] = scale_ref[pl.ds(position()[5], 1), :]
     for b in range(GROUP):
         seeded = jnp.where(seeded_block(seeds_ref, b), scale_ref[b : b + 1, :], 0.0)
@@ -293,8 +293,10 @@
     )(embeddings, tile_list.reshape(-1, 2).T)
     others = []
     for axis in PLANE:
-        for step in (1, 2, 3):
-            others.append(lax.ppermute(bits, axis, pairs(4, step)))
+        near = lax.ppermute(bits, axis, pairs(4, 1))
+        last = lax.ppermute(bits, axis, pairs(4, 3))
+        passed = lax.ppermute(near, axis, pairs(4, 3))
+        others += [near, passed, last]
     plane = exchange(copies, PLANE)
     block = call(
         relay_kernel,
@@ -314,7 +316,7 @@
         (
             array(BLOCKS, ROWS, ROWS, dtype=jnp.bfloat16),
             array(8, BLOCKS, dtype=jnp.int32),
-            array(GROUP, ROWS),
+            array(GROUP, ROWS, dtype=jnp.bfloat16),
             array(GROUP, ROWS, dtype=jnp.int32),
         ),
         [VMEM] + [ANY] * 4,

time: 191 us -> 193 us (1.010)
  waiting for transfers between devices: 49.1 us -> 57.4 us
  starting transfers between devices: 24.6 us -> 21 us
  blocking collectives: 98.9 us -> 96.2 us
    ppermute x6, waiting for transfers between devices: 26.1 us -> 32.8 us  [the longest x2 31.3 us: local(): near = lax.ppermute(bits, axis, pairs(4, 1))]
    all_to_all x6, blocking collectives: 77.6 us -> 73.9 us  [exchange(): return lax.all_to_all(blocks, axes, 0, 0)]
    ppermute x6, starting transfers between devices: 15.6 us -> 13.6 us  [the longest x2 6.02 us: local(): passed = lax.ppermute(near, axis, pairs(4, 3))]
where the time goes in v1:
time: 193 us
  blocking collectives  96.2 us (50%)
  waiting for transfers between devices  57.4 us (30%)
  starting transfers between devices  21 us (11%)
  Pallas kernels  16 us (8%)
    all_to_all x6, blocking collectives, exchange(): return lax.all_to_all(blocks, axes, 0, 0)  73.9 us
    ppermute x2, waiting for transfers between devices, local(): near = lax.ppermute(bits, axis, pairs(4, 1))  31.3 us
    all_gather x1, blocking collectives, local(): lax.all_gather(block, 'zhi')  22.4 us
    ppermute x1, waiting for transfers between devices, local(): far = lax.ppermute(own, 'zlo', pairs(2, 1))  18.2 us
    pallas_call x1, Pallas kernels, local(): call(build_kernel, (array(BLOCKS, ROWS, ROWS, dtype=jnp.bfloat16), array(...  7.47 us
    all_to_all x1, starting transfers between devices, exchange(): return lax.all_to_all(blocks, axes, 0, 0)  7.18 us
    ppermute x2, starting transfers between devices, local(): passed = lax.ppermute(near, axis, pairs(4, 3))  6.02 us
    ppermute x2, starting transfers between devices, local(): last = lax.ppermute(bits, axis, pairs(4, 3))  4.14 us
  transfers between devices with their start and end apart: 12, of which 8 were waited for; matrix products, arithmetic and copies ran while one was open for 0% of the time, Pallas kernels for 0%

profile of v1, /device:TPU:32, one launch (start us, length us, event | category | flops | bytes accessed | tf_op | source)
XLA Modules:
  0.0 192.5 jit_solution(5914295085743099871)
XLA Ops:
  0.0 3.5 %shard_map.37 = (bf16[768,128]{1,0:T(8,128)(2,1)}, bf16[16,768,128]{2,1,0:T(8,128)(2,1)}, bf16[8,128]{1,0:T(8,128)(2,1)}) custom-call(bf16[128,768]{1,0:T(8,128)(2,1)} %emb_hbm.1, s32[2,32]{1,0:T(2,128)} %bitcast.19), custom_call_target="tpu_custom_call" | custom-call | tf_op jit(solution)/shard_map/pallas_call | solution.py:275
  3.5 0.0 copy-start.1
  3.5 0.0 copy-start
  3.5 0.0 copy-start.2
  3.5 7.2 %all-to-all-start = ((bf16[16,768,128]{2,1,0:T(8,128)(2,1)}), bf16[16,768,128]{2,1,0:T(8,128)(2,1)S(1)}, u32[]{:S(2)}, u32[]{:S(2)}) async-start(bf16[16,768,128]{2,1,0:T(8,128)(2,1)} %get-tuple-element.26), calls=%async_computation | async-start | bytes 6291456 | tf_op jit(solution)/shard_map/all_to_all | solution.py:263
  10.7 0.0 copy-done.1
  10.7 2.0 %collective-permute-start.3 = (bf16[8,128]{1,0:T(8,128)(2,1)S(1)}, bf16[8,128]{1,0:T(8,128)(2,1)S(1)}, u32[]{:S(2)}, u32[]{:S(2)}) collective-permute-start(bf16[8,128]{1,0:T(8,128)(2,1)S(1)} %copy-done.1), channel_id=1, source_target_pairs={{0,1},{1,0},{2,3},{3,2},{4,5},{5,4},{6,7},{7,6},{8,9},{9,8},{10,11... | collective-permute-start | bytes 6152 | tf_op jit(solution)/shard_map/ppermute | solution.py:296
  12.7 1.5 collective-permute-start
  14.2 2.1 %collective-permute-start.5 = (bf16[8,128]{1,0:T(8,128)(2,1)S(1)}, bf16[8,128]{1,0:T(8,128)(2,1)S(1)}, u32[]{:S(2)}, u32[]{:S(2)}) collective-permute-start(bf16[8,128]{1,0:T(8,128)(2,1)S(1)} %copy-done.1), channel_id=1, source_target_pairs={{0,3},{1,2},{2,1},{3,0},{4,7},{5,6},{6,5},{7,4},{8,11},{9,10},{10,... | collective-permute-start | bytes 6152 | tf_op jit(solution)/shard_map/ppermute | solution.py:297
  16.3 2.1 %collective-permute-start.2 = (bf16[8,128]{1,0:T(8,128)(2,1)S(1)}, bf16[8,128]{1,0:T(8,128)(2,1)S(1)}, u32[]{:S(2)}, u32[]{:S(2)}) collective-permute-start(bf16[8,128]{1,0:T(8,128)(2,1)S(1)} %copy-done.1), channel_id=1, source_target_pairs={{0,96},{32,64},{64,32},{96,0},{1,97},{33,65},{65,33},{97,1},{2,98}... | collective-permute-start | bytes 6152 | tf_op jit(solution)/shard_map/ppermute | solution.py:297
  18.4 19.0 %collective-permute-done.3.refs_3_ = bf16[8,128]{1,0:T(8,128)(2,1)S(1)} collective-permute-done((bf16[8,128]{1,0:T(8,128)(2,1)S(1)}, bf16[8,128]{1,0:T(8,128)(2,1)S(1)}, u32[]{:S(2)}, u32[]{:S(2)}) %collective-permute-start.3) | collective-permute-done | bytes 2080 | tf_op jit(solution)/shard_map/ppermute | solution.py:296
  37.4 0.0 collective-permute-start.4
  37.4 12.2 %collective-permute-done.refs_0_ = bf16[8,128]{1,0:T(8,128)(2,1)S(1)} collective-permute-done((bf16[8,128]{1,0:T(8,128)(2,1)S(1)}, bf16[8,128]{1,0:T(8,128)(2,1)S(1)}, u32[]{:S(2)}, u32[]{:S(2)}) %collective-permute-start) | collective-permute-done | bytes 2080 | tf_op jit(solution)/shard_map/ppermute | solution.py:296
  49.6 6.0 %collective-permute-start.1 = (bf16[8,128]{1,0:T(8,128)(2,1)S(1)}, bf16[8,128]{1,0:T(8,128)(2,1)S(1)}, u32[]{:S(2)}, u32[]{:S(2)}) collective-permute-start(bf16[8,128]{1,0:T(8,128)(2,1)S(1)} %collective-permute-done.refs_0_), channel_id=1, source_target_pairs={{0,96},{32,64},{64,32},{96,0},{1,97},{33,65},{65,33},{97,1},{2,98}... | collective-permute-start | bytes 6152 | tf_op jit(solution)/shard_map/ppermute | solution.py:298
  55.7 0.0 collective-permute-done.5.refs_5_
  55.7 0.0 collective-permute-done.2.refs_2_
  55.7 0.0 collective-permute-done.4.refs_4_
  55.7 1.5 collective-permute-done.1.refs_1_
  57.2 0.0 copy-done
  57.2 0.0 copy-done.2
  57.3 22.4 %all-gather = bf16[3168,128]{1,0:T(8,128)(2,1)S(1)} all-gather(bf16[792,128]{1,0:T(8,128)(2,1)S(1)} %shard_map.38), channel_id=2, replica_groups=mesh['zlo'=2,'x'=4,'core'=2,'zhi'=4,'y'=4] {'zhi'}, dimensions={0}, use_global_device_ids=true | all-gather | bytes 1013760 | tf_op jit(solution)/shard_map/all_gather | solution.py:308
  79.6 0.0 copy-start.3
  79.6 0.0 collective-permute-start.7
  79.6 0.2 collective-permute-start.6
  79.8 2.1 %collective-permute-done.7.mate_ref = bf16[4,792,128]{2,1,0:T(8,128)(2,1)S(1)} collective-permute-done((bf16[4,792,128]{2,1,0:T(8,128)(2,1)S(1)}, bf16[4,792,128]{2,1,0:T(8,128)(2,1)S(1)}, u32[]{:S(2)}, u32[]{:S(2)}) %collective-permute-start.7) | collective-permute-done | bytes 811040 | tf_op jit(solution)/shard_map/ppermute | solution.py:310
  82.0 0.0 copy-start.4
  82.0 18.2 %collective-permute-done.6.far_ref = bf16[4,792,128]{2,1,0:T(8,128)(2,1)S(1)} collective-permute-done((bf16[4,792,128]{2,1,0:T(8,128)(2,1)S(1)}, bf16[4,792,128]{2,1,0:T(8,128)(2,1)S(1)}, u32[]{:S(2)}, u32[]{:S(2)}) %collective-permute-start.6) | collective-permute-done | bytes 811040 | tf_op jit(solution)/shard_map/ppermute | solution.py:309
  100.1 0.0 collective-permute-start.8
  100.1 0.0 copy-done.3
  100.1 0.0 copy-done.4
  100.1 0.9 copy-done.5
  101.0 1.5 collective-permute-done.8.far_mate_ref
  102.6 0.0 all-to-all-done.plane_ref
  102.6 7.5 %shard_map.39 = (bf16[256,128,128]{2,1,0:T(8,128)(2,1)S(1)}, s32[8,256]{1,0:T(8,128)S(1)}, bf16[16,128]{1,0:T(8,128)(2,1)S(1)}, s32[16,128]{1,0:T(8,128)S(1)}) custom-call(bf16[16,768,128]{2,1,0:T(8,128)(2,1)S(1)} %all-to-all-done.plane_ref, bf16[4,792,128]{2,1,0:T(8,128)(2,1)} %bitcast.18, bf16[4,792,128]{2,1,0:T(8,128)(2,1)} %copy-done.4, ...), custom_call_target="tpu_custom_call" | custom-call | tf_op jit(solution)/shard_map/pallas_call | solution.py:314
  110.1 11.0 %all_to_all.35.parts_ref = bf16[16,16,128]{2,1,0:T(8,128)(2,1)S(1)} all-to-all(bf16[16,16,128]{2,1,0:T(8,128)(2,1)S(1)} %broadcast_in_dim.9), channel_id=1, replica_groups=mesh['zlo'=2,'x'=4,'core'=2,'zhi'=4,'y'=4] {'zlo','core','zhi'}, dimensions={0} | all-to-all | bytes 131072 | tf_op jit(solution)/shard_map/all_to_all | solution.py:263
  121.1 1.6 shard_map.40
  122.7 15.8 %all_to_all.36 = bf16[16,64,128]{2,1,0:T(8,128)(2,1)S(1)} all-to-all(bf16[16,64,128]{2,1,0:T(8,128)(2,1)S(1)} %get-tuple-element.36), channel_id=1, replica_groups=mesh['zlo'=2,'x'=4,'core'=2,'zhi'=4,'y'=4] {'x','y'}, dimensions={0} | all-to-all | bytes 524288 | tf_op jit(solution)/shard_map/all_to_all | solution.py:263
  138.6 11.0 %all_to_all.37.own_ref = bf16[8,64,128]{2,1,0:T(8,128)(2,1)S(1)} all-to-all(bf16[8,64,128]{2,1,0:T(8,128)(2,1)S(1)} %broadcast_in_dim.10), channel_id=1, replica_groups=mesh['zlo'=2,'x'=4,'core'=2,'zhi'=4,'y'=4] {'zlo','zhi'}, dimensions={0} | all-to-all | bytes 262144 | tf_op jit(solution)/shard_map/all_to_all | solution.py:263
  149.7 0.0 collective-permute-start.9
  149.7 1.3 collective-permute-done.9.mate_ref
  151.0 1.7 shard_map.41
  152.7 12.7 %all_to_all.38 = bf16[16,64,128]{2,1,0:T(8,128)(2,1)S(1)} all-to-all(bf16[16,64,128]{2,1,0:T(8,128)(2,1)S(1)} %shard_map.41), channel_id=1, replica_groups=mesh['zlo'=2,'x'=4,'core'=2,'zhi'=4,'y'=4] {'x','y'}, dimensions={0} | all-to-all | bytes 524288 | tf_op jit(solution)/shard_map/all_to_all | solution.py:263
  165.4 10.7 %all_to_all.39.own_ref = bf16[8,64,128]{2,1,0:T(8,128)(2,1)S(1)} all-to-all(bf16[8,64,128]{2,1,0:T(8,128)(2,1)S(1)} %broadcast_in_dim.11), channel_id=1, replica_groups=mesh['zlo'=2,'x'=4,'core'=2,'zhi'=4,'y'=4] {'zlo','zhi'}, dimensions={0} | all-to-all | bytes 262144 | tf_op jit(solution)/shard_map/all_to_all | solution.py:263
  176.2 0.0 collective-permute-start.10
  176.2 1.3 collective-permute-done.10.mate_ref
  177.5 1.7 shard_map.42
  179.2 12.7 %all_to_all.40 = bf16[16,64,128]{2,1,0:T(8,128)(2,1)S(1)} all-to-all(bf16[16,64,128]{2,1,0:T(8,128)(2,1)S(1)} %shard_map.42), channel_id=1, replica_groups=mesh['zlo'=2,'x'=4,'core'=2,'zhi'=4,'y'=4] {'x','y'}, dimensions={0} | all-to-all | bytes 524288 | tf_op jit(solution)/shard_map/all_to_all | solution.py:263
  191.9 0.6 fusion
  (13 shorter events, 0.2 us)
Async XLA Ops:
  3.5 7.2 %copy-start.1 = (bf16[8,128]{1,0:T(8,128)(2,1)S(1)}, bf16[8,128]{1,0:T(8,128)(2,1)}, u32[]{:S(2)}) copy-start(bf16[8,128]{1,0:T(8,128)(2,1)} %get-tuple-element.28.bits_ref) | copy-start | bytes 6148
  3.5 53.7 %copy-start = (bf16[768,128]{1,0:T(8,128)(2,1)S(1)}, bf16[768,128]{1,0:T(8,128)(2,1)}, u32[]{:S(2)}) copy-start(bf16[768,128]{1,0:T(8,128)(2,1)} %get-tuple-element.27.folded_ref) | copy-start | bytes 589828
  3.5 53.7 %copy-start.2 = (s32[128]{0:T(128)S(1)}, s32[128]{0:T(128)}, u32[]{:S(2)}) copy-start(s32[128]{0:T(128)} %param.5) | copy-start | bytes 1540
  3.5 99.0 %all-to-all-start = ((bf16[16,768,128]{2,1,0:T(8,128)(2,1)}), bf16[16,768,128]{2,1,0:T(8,128)(2,1)S(1)}, u32[]{:S(2)}, u32[]{:S(2)}) async-start(bf16[16,768,128]{2,1,0:T(8,128)(2,1)} %get-tuple-element.26), calls=%async_computation | async-start | bytes 6291456 | tf_op jit(solution)/shard_map/all_to_all | solution.py:263
  10.7 26.7 %collective-permute-start.3 = (bf16[8,128]{1,0:T(8,128)(2,1)S(1)}, bf16[8,128]{1,0:T(8,128)(2,1)S(1)}, u32[]{:S(2)}, u32[]{:S(2)}) collective-permute-start(bf16[8,128]{1,0:T(8,128)(2,1)S(1)} %copy-done.1), channel_id=1, source_target_pairs={{0,1},{1,0},{2,3},{3,2},{4,5},{5,4},{6,7},{7,6},{8,9},{9,8},{10,11... | collective-permute-start | bytes 6152 | tf_op jit(solution)/shard_map/ppermute | solution.py:296
  12.7 36.9 %collective-permute-start = (bf16[8,128]{1,0:T(8,128)(2,1)S(1)}, bf16[8,128]{1,0:T(8,128)(2,1)S(1)}, u32[]{:S(2)}, u32[]{:S(2)}) collective-permute-start(bf16[8,128]{1,0:T(8,128)(2,1)S(1)} %copy-done.1), channel_id=1, source_target_pairs={{0,32},{32,0},{64,96},{96,64},{1,33},{33,1},{65,97},{97,65},{2,34}... | collective-permute-start | bytes 6152 | tf_op jit(solution)/shard_map/ppermute | solution.py:296
  14.2 41.5 %collective-permute-start.5 = (bf16[8,128]{1,0:T(8,128)(2,1)S(1)}, bf16[8,128]{1,0:T(8,128)(2,1)S(1)}, u32[]{:S(2)}, u32[]{:S(2)}) collective-permute-start(bf16[8,128]{1,0:T(8,128)(2,1)S(1)} %copy-done.1), channel_id=1, source_target_pairs={{0,3},{1,2},{2,1},{3,0},{4,7},{5,6},{6,5},{7,4},{8,11},{9,10},{10,... | collective-permute-start | bytes 6152 | tf_op jit(solution)/shard_map/ppermute | solution.py:297
  16.3 39.4 %collective-permute-start.2 = (bf16[8,128]{1,0:T(8,128)(2,1)S(1)}, bf16[8,128]{1,0:T(8,128)(2,1)S(1)}, u32[]{:S(2)}, u32[]{:S(2)}) collective-permute-start(bf16[8,128]{1,0:T(8,128)(2,1)S(1)} %copy-done.1), channel_id=1, source_target_pairs={{0,96},{32,64},{64,32},{96,0},{1,97},{33,65},{65,33},{97,1},{2,98}... | collective-permute-start | bytes 6152 | tf_op jit(solution)/shard_map/ppermute | solution.py:297
  37.4 18.3 %collective-permute-start.4 = (bf16[8,128]{1,0:T(8,128)(2,1)S(1)}, bf16[8,128]{1,0:T(8,128)(2,1)S(1)}, u32[]{:S(2)}, u32[]{:S(2)}) collective-permute-start(bf16[8,128]{1,0:T(8,128)(2,1)S(1)} %collective-permute-done.3.refs_3_), channel_id=1, source_target_pairs={{0,3},{1,2},{2,1},{3,0},{4,7},{5,6},{6,5},{7,4},{8,11},{9,10},{10,... | collective-permute-start | bytes 6152 | tf_op jit(solution)/shard_map/ppermute | solution.py:298
  49.6 7.6 %collective-permute-start.1 = (bf16[8,128]{1,0:T(8,128)(2,1)S(1)}, bf16[8,128]{1,0:T(8,128)(2,1)S(1)}, u32[]{:S(2)}, u32[]{:S(2)}) collective-permute-start(bf16[8,128]{1,0:T(8,128)(2,1)S(1)} %collective-permute-done.refs_0_), channel_id=1, source_target_pairs={{0,96},{32,64},{64,32},{96,0},{1,97},{33,65},{65,33},{97,1},{2,98}... | collective-permute-start | bytes 6152 | tf_op jit(solution)/shard_map/ppermute | solution.py:298
  79.6 20.5 %copy-start.3 = (bf16[3168,128]{1,0:T(8,128)(2,1)}, bf16[3168,128]{1,0:T(8,128)(2,1)S(1)}, u32[]{:S(2)}) copy-start(bf16[3168,128]{1,0:T(8,128)(2,1)S(1)} %all-gather) | copy-start | bytes 2433028
  79.6 2.3 %collective-permute-start.7 = (bf16[4,792,128]{2,1,0:T(8,128)(2,1)S(1)}, bf16[4,792,128]{2,1,0:T(8,128)(2,1)S(1)}, u32[]{:S(2)}, u32[]{:S(2)}) collective-permute-start(bf16[4,792,128]{2,1,0:T(8,128)(2,1)S(1)} %bitcast.16), channel_id=1, source_target_pairs={{0,16},{16,0},{1,17},{17,1},{2,18},{18,2},{3,19},{19,3},{4,20},{20... | collective-permute-start | bytes 2433032 | tf_op jit(solution)/shard_map/ppermute | solution.py:310
  79.6 20.5 %collective-permute-start.6 = (bf16[4,792,128]{2,1,0:T(8,128)(2,1)S(1)}, bf16[4,792,128]{2,1,0:T(8,128)(2,1)S(1)}, u32[]{:S(2)}, u32[]{:S(2)}) collective-permute-start(bf16[4,792,128]{2,1,0:T(8,128)(2,1)S(1)} %bitcast.17), channel_id=1, source_target_pairs={{0,128},{128,0},{1,129},{129,1},{2,130},{130,2},{3,131},{131,3},{4... | collective-permute-start | bytes 2433032 | tf_op jit(solution)/shard_map/ppermute | solution.py:309
  82.0 18.2 %copy-start.4 = (bf16[4,792,128]{2,1,0:T(8,128)(2,1)}, bf16[4,792,128]{2,1,0:T(8,128)(2,1)S(1)}, u32[]{:S(2)}) copy-start(bf16[4,792,128]{2,1,0:T(8,128)(2,1)S(1)} %collective-permute-done.7.mate_ref) | copy-start | bytes 2433028
  100.1 0.9 copy-start.5
  100.1 2.5 %collective-permute-start.8 = (bf16[4,792,128]{2,1,0:T(8,128)(2,1)S(1)}, bf16[4,792,128]{2,1,0:T(8,128)(2,1)}, u32[]{:S(2)}, u32[]{:S(2)}) collective-permute-start(bf16[4,792,128]{2,1,0:T(8,128)(2,1)S(1)} %collective-permute-done.6.far_ref), channel_id=1, source_target_pairs={{0,16},{16,0},{1,17},{17,1},{2,18},{18,2},{3,19},{19,3},{4,20},{20... | collective-permute-start | bytes 2433032 | tf_op jit(solution)/shard_map/ppermute | solution.py:312
  149.7 1.3 collective-permute-start.9
  176.2 1.3 collective-permute-start.10

commit v2 on v1

--- a/solution.py
+++ b/solution.py
@@ -196,7 +196,16 @@
     tile = jnp.where(off_diag, tile, 0.0)
     tiles_ref[list_ref[3, 0]] = tile.astype(jnp.bfloat16)
     sums[mine] += tile
-    rows = [jnp.sum(sums[b].T, axis=0, keepdims=True) for b in range(GROUP)]
+    ones = jnp.ones((8, 2 * ROWS), jnp.bfloat16)
+    rows = []
+    for b in range(GROUP):
+        high = sums[b].astype(jnp.bfloat16)
+        low = (sums[b] - high.astype(jnp.float32)).astype(jnp.bfloat16)
+        row = lax.dot_general(
+            ones, jnp.concatenate([high, low], axis=1), (((1,), (1,)), ((), ())),
+            preferred_element_type=jnp.float32,
+        )
+        rows.append(row[0:1])
     deg_ref[...] = jnp.concatenate(rows, axis=0).astype(jnp.bfloat16)
 
 

time: 193 us -> 193 us (level)
  no operation moved by 1% of the time
where the time goes in v2:
time: 193 us
  blocking collectives  96.2 us (50%)
  waiting for transfers between devices  57.4 us (30%)
  starting transfers between devices  21 us (11%)
  Pallas kernels  16 us (8%)
    all_to_all x6, blocking collectives, exchange(): return lax.all_to_all(blocks, axes, 0, 0)  73.9 us
    ppermute x2, waiting for transfers between devices, local(): near = lax.ppermute(bits, axis, pairs(4, 1))  31.3 us
    all_gather x1, blocking collectives, local(): lax.all_gather(block, 'zhi')  22.4 us
    ppermute x1, waiting for transfers between devices, local(): far = lax.ppermute(own, 'zlo', pairs(2, 1))  18.2 us
    pallas_call x1, Pallas kernels, local(): call(build_kernel, (array(BLOCKS, ROWS, ROWS, dtype=jnp.bfloat16), array(...  7.47 us
    all_to_all x1, starting transfers between devices, exchange(): return lax.all_to_all(blocks, axes, 0, 0)  7.18 us
    ppermute x2, starting transfers between devices, local(): passed = lax.ppermute(near, axis, pairs(4, 3))  6.02 us
    ppermute x2, starting transfers between devices, local(): last = lax.ppermute(bits, axis, pairs(4, 3))  4.14 us
  transfers between devices with their start and end apart: 12, of which 8 were waited for; matrix products, arithmetic and copies ran while one was open for 0% of the time, Pallas kernels for 0%

profile of v2, /device:TPU:32, one launch (start us, length us, event | category | flops | bytes accessed | tf_op | source)
XLA Modules:
  0.0 192.5 jit_solution(17579978567195668637)
XLA Ops:
  0.0 3.5 %shard_map.37 = (bf16[768,128]{1,0:T(8,128)(2,1)}, bf16[16,768,128]{2,1,0:T(8,128)(2,1)}, bf16[8,128]{1,0:T(8,128)(2,1)}) custom-call(bf16[128,768]{1,0:T(8,128)(2,1)} %emb_hbm.1, s32[2,32]{1,0:T(2,128)} %bitcast.19), custom_call_target="tpu_custom_call" | custom-call | tf_op jit(solution)/shard_map/pallas_call | solution.py:284
  3.5 0.0 copy-start.1
  3.5 0.0 copy-start
  3.5 0.0 copy-start.2
  3.5 7.2 %all-to-all-start = ((bf16[16,768,128]{2,1,0:T(8,128)(2,1)}), bf16[16,768,128]{2,1,0:T(8,128)(2,1)S(1)}, u32[]{:S(2)}, u32[]{:S(2)}) async-start(bf16[16,768,128]{2,1,0:T(8,128)(2,1)} %get-tuple-element.26), calls=%async_computation | async-start | bytes 6291456 | tf_op jit(solution)/shard_map/all_to_all | solution.py:272
  10.7 0.0 copy-done.1
  10.7 2.0 %collective-permute-start.3 = (bf16[8,128]{1,0:T(8,128)(2,1)S(1)}, bf16[8,128]{1,0:T(8,128)(2,1)S(1)}, u32[]{:S(2)}, u32[]{:S(2)}) collective-permute-start(bf16[8,128]{1,0:T(8,128)(2,1)S(1)} %copy-done.1), channel_id=1, source_target_pairs={{0,1},{1,0},{2,3},{3,2},{4,5},{5,4},{6,7},{7,6},{8,9},{9,8},{10,11... | collective-permute-start | bytes 6152 | tf_op jit(solution)/shard_map/ppermute | solution.py:305
  12.7 1.5 collective-permute-start
  14.2 2.1 %collective-permute-start.5 = (bf16[8,128]{1,0:T(8,128)(2,1)S(1)}, bf16[8,128]{1,0:T(8,128)(2,1)S(1)}, u32[]{:S(2)}, u32[]{:S(2)}) collective-permute-start(bf16[8,128]{1,0:T(8,128)(2,1)S(1)} %copy-done.1), channel_id=1, source_target_pairs={{0,3},{1,2},{2,1},{3,0},{4,7},{5,6},{6,5},{7,4},{8,11},{9,10},{10,... | collective-permute-start | bytes 6152 | tf_op jit(solution)/shard_map/ppermute | solution.py:306
  16.3 2.1 %collective-permute-start.2 = (bf16[8,128]{1,0:T(8,128)(2,1)S(1)}, bf16[8,128]{1,0:T(8,128)(2,1)S(1)}, u32[]{:S(2)}, u32[]{:S(2)}) collective-permute-start(bf16[8,128]{1,0:T(8,128)(2,1)S(1)} %copy-done.1), channel_id=1, source_target_pairs={{0,96},{32,64},{64,32},{96,0},{1,97},{33,65},{65,33},{97,1},{2,98}... | collective-permute-start | bytes 6152 | tf_op jit(solution)/shard_map/ppermute | solution.py:306
  18.4 19.0 %collective-permute-done.3.refs_3_ = bf16[8,128]{1,0:T(8,128)(2,1)S(1)} collective-permute-done((bf16[8,128]{1,0:T(8,128)(2,1)S(1)}, bf16[8,128]{1,0:T(8,128)(2,1)S(1)}, u32[]{:S(2)}, u32[]{:S(2)}) %collective-permute-start.3) | collective-permute-done | bytes 2080 | tf_op jit(solution)/shard_map/ppermute | solution.py:305
  37.4 0.0 collective-permute-start.4
  37.4 12.2 %collective-permute-done.refs_0_ = bf16[8,128]{1,0:T(8,128)(2,1)S(1)} collective-permute-done((bf16[8,128]{1,0:T(8,128)(2,1)S(1)}, bf16[8,128]{1,0:T(8,128)(2,1)S(1)}, u32[]{:S(2)}, u32[]{:S(2)}) %collective-permute-start) | collective-permute-done | bytes 2080 | tf_op jit(solution)/shard_map/ppermute | solution.py:305
  49.6 6.0 %collective-permute-start.1 = (bf16[8,128]{1,0:T(8,128)(2,1)S(1)}, bf16[8,128]{1,0:T(8,128)(2,1)S(1)}, u32[]{:S(2)}, u32[]{:S(2)}) collective-permute-start(bf16[8,128]{1,0:T(8,128)(2,1)S(1)} %collective-permute-done.refs_0_), channel_id=1, source_target_pairs={{0,96},{32,64},{64,32},{96,0},{1,97},{33,65},{65,33},{97,1},{2,98}... | collective-permute-start | bytes 6152 | tf_op jit(solution)/shard_map/ppermute | solution.py:307
  55.7 0.0 collective-permute-done.5.refs_5_
  55.7 0.0 collective-permute-done.2.refs_2_
  55.7 0.0 collective-permute-done.4.refs_4_
  55.7 1.5 collective-permute-done.1.refs_1_
  57.2 0.0 copy-done
  57.2 0.0 copy-done.2
  57.3 22.4 %all-gather = bf16[3168,128]{1,0:T(8,128)(2,1)S(1)} all-gather(bf16[792,128]{1,0:T(8,128)(2,1)S(1)} %shard_map.38), channel_id=2, replica_groups=mesh['zlo'=2,'x'=4,'core'=2,'zhi'=4,'y'=4] {'zhi'}, dimensions={0}, use_global_device_ids=true | all-gather | bytes 1013760 | tf_op jit(solution)/shard_map/all_gather | solution.py:317
  79.6 0.0 copy-start.3
  79.6 0.0 collective-permute-start.7
  79.6 0.2 collective-permute-start.6
  79.8 2.1 %collective-permute-done.7.mate_ref = bf16[4,792,128]{2,1,0:T(8,128)(2,1)S(1)} collective-permute-done((bf16[4,792,128]{2,1,0:T(8,128)(2,1)S(1)}, bf16[4,792,128]{2,1,0:T(8,128)(2,1)S(1)}, u32[]{:S(2)}, u32[]{:S(2)}) %collective-permute-start.7) | collective-permute-done | bytes 811040 | tf_op jit(solution)/shard_map/ppermute | solution.py:319
  82.0 0.0 copy-start.4
  82.0 18.2 %collective-permute-done.6.far_ref = bf16[4,792,128]{2,1,0:T(8,128)(2,1)S(1)} collective-permute-done((bf16[4,792,128]{2,1,0:T(8,128)(2,1)S(1)}, bf16[4,792,128]{2,1,0:T(8,128)(2,1)S(1)}, u32[]{:S(2)}, u32[]{:S(2)}) %collective-permute-start.6) | collective-permute-done | bytes 811040 | tf_op jit(solution)/shard_map/ppermute | solution.py:318
  100.1 0.0 collective-permute-start.8
  100.1 0.0 copy-done.3
  100.1 0.0 copy-done.4
  100.1 0.9 copy-done.5
  101.0 1.5 collective-permute-done.8.far_mate_ref
  102.6 0.0 all-to-all-done.plane_ref
  102.6 7.5 %shard_map.39 = (bf16[256,128,128]{2,1,0:T(8,128)(2,1)S(1)}, s32[8,256]{1,0:T(8,128)S(1)}, bf16[16,128]{1,0:T(8,128)(2,1)S(1)}, s32[16,128]{1,0:T(8,128)S(1)}) custom-call(bf16[16,768,128]{2,1,0:T(8,128)(2,1)S(1)} %all-to-all-done.plane_ref, bf16[4,792,128]{2,1,0:T(8,128)(2,1)} %bitcast.18, bf16[4,792,128]{2,1,0:T(8,128)(2,1)} %copy-done.4, ...), custom_call_target="tpu_custom_call" | custom-call | tf_op jit(solution)/shard_map/pallas_call | solution.py:323
  110.1 11.0 %all_to_all.35.parts_ref = bf16[16,16,128]{2,1,0:T(8,128)(2,1)S(1)} all-to-all(bf16[16,16,128]{2,1,0:T(8,128)(2,1)S(1)} %broadcast_in_dim.9), channel_id=1, replica_groups=mesh['zlo'=2,'x'=4,'core'=2,'zhi'=4,'y'=4] {'zlo','core','zhi'}, dimensions={0} | all-to-all | bytes 131072 | tf_op jit(solution)/shard_map/all_to_all | solution.py:272
  121.1 1.6 shard_map.40
  122.7 15.8 %all_to_all.36 = bf16[16,64,128]{2,1,0:T(8,128)(2,1)S(1)} all-to-all(bf16[16,64,128]{2,1,0:T(8,128)(2,1)S(1)} %get-tuple-element.36), channel_id=1, replica_groups=mesh['zlo'=2,'x'=4,'core'=2,'zhi'=4,'y'=4] {'x','y'}, dimensions={0} | all-to-all | bytes 524288 | tf_op jit(solution)/shard_map/all_to_all | solution.py:272
  138.6 11.0 %all_to_all.37.own_ref = bf16[8,64,128]{2,1,0:T(8,128)(2,1)S(1)} all-to-all(bf16[8,64,128]{2,1,0:T(8,128)(2,1)S(1)} %broadcast_in_dim.10), channel_id=1, replica_groups=mesh['zlo'=2,'x'=4,'core'=2,'zhi'=4,'y'=4] {'zlo','zhi'}, dimensions={0} | all-to-all | bytes 262144 | tf_op jit(solution)/shard_map/all_to_all | solution.py:272
  149.7 0.0 collective-permute-start.9
  149.7 1.3 collective-permute-done.9.mate_ref
  151.0 1.7 shard_map.41
  152.7 12.7 %all_to_all.38 = bf16[16,64,128]{2,1,0:T(8,128)(2,1)S(1)} all-to-all(bf16[16,64,128]{2,1,0:T(8,128)(2,1)S(1)} %shard_map.41), channel_id=1, replica_groups=mesh['zlo'=2,'x'=4,'core'=2,'zhi'=4,'y'=4] {'x','y'}, dimensions={0} | all-to-all | bytes 524288 | tf_op jit(solution)/shard_map/all_to_all | solution.py:272
  165.4 10.7 %all_to_all.39.own_ref = bf16[8,64,128]{2,1,0:T(8,128)(2,1)S(1)} all-to-all(bf16[8,64,128]{2,1,0:T(8,128)(2,1)S(1)} %broadcast_in_dim.11), channel_id=1, replica_groups=mesh['zlo'=2,'x'=4,'core'=2,'zhi'=4,'y'=4] {'zlo','zhi'}, dimensions={0} | all-to-all | bytes 262144 | tf_op jit(solution)/shard_map/all_to_all | solution.py:272
  176.2 0.0 collective-permute-start.10
  176.2 1.3 collective-permute-done.10.mate_ref
  177.5 1.7 shard_map.42
  179.2 12.7 %all_to_all.40 = bf16[16,64,128]{2,1,0:T(8,128)(2,1)S(1)} all-to-all(bf16[16,64,128]{2,1,0:T(8,128)(2,1)S(1)} %shard_map.42), channel_id=1, replica_groups=mesh['zlo'=2,'x'=4,'core'=2,'zhi'=4,'y'=4] {'x','y'}, dimensions={0} | all-to-all | bytes 524288 | tf_op jit(solution)/shard_map/all_to_all | solution.py:272
  191.9 0.6 fusion
  (13 shorter events, 0.2 us)
Async XLA Ops:
  3.5 7.2 %copy-start.1 = (bf16[8,128]{1,0:T(8,128)(2,1)S(1)}, bf16[8,128]{1,0:T(8,128)(2,1)}, u32[]{:S(2)}) copy-start(bf16[8,128]{1,0:T(8,128)(2,1)} %get-tuple-element.28.bits_ref) | copy-start | bytes 6148
  3.5 53.7 %copy-start = (bf16[768,128]{1,0:T(8,128)(2,1)S(1)}, bf16[768,128]{1,0:T(8,128)(2,1)}, u32[]{:S(2)}) copy-start(bf16[768,128]{1,0:T(8,128)(2,1)} %get-tuple-element.27.folded_ref) | copy-start | bytes 589828
  3.5 53.7 %copy-start.2 = (s32[128]{0:T(128)S(1)}, s32[128]{0:T(128)}, u32[]{:S(2)}) copy-start(s32[128]{0:T(128)} %param.5) | copy-start | bytes 1540
  3.5 99.0 %all-to-all-start = ((bf16[16,768,128]{2,1,0:T(8,128)(2,1)}), bf16[16,768,128]{2,1,0:T(8,128)(2,1)S(1)}, u32[]{:S(2)}, u32[]{:S(2)}) async-start(bf16[16,768,128]{2,1,0:T(8,128)(2,1)} %get-tuple-element.26), calls=%async_computation | async-start | bytes 6291456 | tf_op jit(solution)/shard_map/all_to_all | solution.py:272
  10.7 26.7 %collective-permute-start.3 = (bf16[8,128]{1,0:T(8,128)(2,1)S(1)}, bf16[8,128]{1,0:T(8,128)(2,1)S(1)}, u32[]{:S(2)}, u32[]{:S(2)}) collective-permute-start(bf16[8,128]{1,0:T(8,128)(2,1)S(1)} %copy-done.1), channel_id=1, source_target_pairs={{0,1},{1,0},{2,3},{3,2},{4,5},{5,4},{6,7},{7,6},{8,9},{9,8},{10,11... | collective-permute-start | bytes 6152 | tf_op jit(solution)/shard_map/ppermute | solution.py:305
  12.7 36.9 %collective-permute-start = (bf16[8,128]{1,0:T(8,128)(2,1)S(1)}, bf16[8,128]{1,0:T(8,128)(2,1)S(1)}, u32[]{:S(2)}, u32[]{:S(2)}) collective-permute-start(bf16[8,128]{1,0:T(8,128)(2,1)S(1)} %copy-done.1), channel_id=1, source_target_pairs={{0,32},{32,0},{64,96},{96,64},{1,33},{33,1},{65,97},{97,65},{2,34}... | collective-permute-start | bytes 6152 | tf_op jit(solution)/shard_map/ppermute | solution.py:305
  14.2 41.5 %collective-permute-start.5 = (bf16[8,128]{1,0:T(8,128)(2,1)S(1)}, bf16[8,128]{1,0:T(8,128)(2,1)S(1)}, u32[]{:S(2)}, u32[]{:S(2)}) collective-permute-start(bf16[8,128]{1,0:T(8,128)(2,1)S(1)} %copy-done.1), channel_id=1, source_target_pairs={{0,3},{1,2},{2,1},{3,0},{4,7},{5,6},{6,5},{7,4},{8,11},{9,10},{10,... | collective-permute-start | bytes 6152 | tf_op jit(solution)/shard_map/ppermute | solution.py:306
  16.3 39.4 %collective-permute-start.2 = (bf16[8,128]{1,0:T(8,128)(2,1)S(1)}, bf16[8,128]{1,0:T(8,128)(2,1)S(1)}, u32[]{:S(2)}, u32[]{:S(2)}) collective-permute-start(bf16[8,128]{1,0:T(8,128)(2,1)S(1)} %copy-done.1), channel_id=1, source_target_pairs={{0,96},{32,64},{64,32},{96,0},{1,97},{33,65},{65,33},{97,1},{2,98}... | collective-permute-start | bytes 6152 | tf_op jit(solution)/shard_map/ppermute | solution.py:306
  37.4 18.3 %collective-permute-start.4 = (bf16[8,128]{1,0:T(8,128)(2,1)S(1)}, bf16[8,128]{1,0:T(8,128)(2,1)S(1)}, u32[]{:S(2)}, u32[]{:S(2)}) collective-permute-start(bf16[8,128]{1,0:T(8,128)(2,1)S(1)} %collective-permute-done.3.refs_3_), channel_id=1, source_target_pairs={{0,3},{1,2},{2,1},{3,0},{4,7},{5,6},{6,5},{7,4},{8,11},{9,10},{10,... | collective-permute-start | bytes 6152 | tf_op jit(solution)/shard_map/ppermute | solution.py:307
  49.6 7.6 %collective-permute-start.1 = (bf16[8,128]{1,0:T(8,128)(2,1)S(1)}, bf16[8,128]{1,0:T(8,128)(2,1)S(1)}, u32[]{:S(2)}, u32[]{:S(2)}) collective-permute-start(bf16[8,128]{1,0:T(8,128)(2,1)S(1)} %collective-permute-done.refs_0_), channel_id=1, source_target_pairs={{0,96},{32,64},{64,32},{96,0},{1,97},{33,65},{65,33},{97,1},{2,98}... | collective-permute-start | bytes 6152 | tf_op jit(solution)/shard_map/ppermute | solution.py:307
  79.6 20.5 %copy-start.3 = (bf16[3168,128]{1,0:T(8,128)(2,1)}, bf16[3168,128]{1,0:T(8,128)(2,1)S(1)}, u32[]{:S(2)}) copy-start(bf16[3168,128]{1,0:T(8,128)(2,1)S(1)} %all-gather) | copy-start | bytes 2433028
  79.6 2.3 %collective-permute-start.7 = (bf16[4,792,128]{2,1,0:T(8,128)(2,1)S(1)}, bf16[4,792,128]{2,1,0:T(8,128)(2,1)S(1)}, u32[]{:S(2)}, u32[]{:S(2)}) collective-permute-start(bf16[4,792,128]{2,1,0:T(8,128)(2,1)S(1)} %bitcast.16), channel_id=1, source_target_pairs={{0,16},{16,0},{1,17},{17,1},{2,18},{18,2},{3,19},{19,3},{4,20},{20... | collective-permute-start | bytes 2433032 | tf_op jit(solution)/shard_map/ppermute | solution.py:319
  79.6 20.5 %collective-permute-start.6 = (bf16[4,792,128]{2,1,0:T(8,128)(2,1)S(1)}, bf16[4,792,128]{2,1,0:T(8,128)(2,1)S(1)}, u32[]{:S(2)}, u32[]{:S(2)}) collective-permute-start(bf16[4,792,128]{2,1,0:T(8,128)(2,1)S(1)} %bitcast.17), channel_id=1, source_target_pairs={{0,128},{128,0},{1,129},{129,1},{2,130},{130,2},{3,131},{131,3},{4... | collective-permute-start | bytes 2433032 | tf_op jit(solution)/shard_map/ppermute | solution.py:318
  82.0 18.2 %copy-start.4 = (bf16[4,792,128]{2,1,0:T(8,128)(2,1)}, bf16[4,792,128]{2,1,0:T(8,128)(2,1)S(1)}, u32[]{:S(2)}) copy-start(bf16[4,792,128]{2,1,0:T(8,128)(2,1)S(1)} %collective-permute-done.7.mate_ref) | copy-start | bytes 2433028
  100.1 0.9 copy-start.5
  100.1 2.5 %collective-permute-start.8 = (bf16[4,792,128]{2,1,0:T(8,128)(2,1)S(1)}, bf16[4,792,128]{2,1,0:T(8,128)(2,1)}, u32[]{:S(2)}, u32[]{:S(2)}) collective-permute-start(bf16[4,792,128]{2,1,0:T(8,128)(2,1)S(1)} %collective-permute-done.6.far_ref), channel_id=1, source_target_pairs={{0,16},{16,0},{1,17},{17,1},{2,18},{18,2},{3,19},{19,3},{4,20},{20... | collective-permute-start | bytes 2433032 | tf_op jit(solution)/shard_map/ppermute | solution.py:321
  149.7 1.3 collective-permute-start.9
  176.2 1.3 collective-permute-start.10
